TPU v7x, 32 devices: a whole 2x2x4 slice. The times are simulated.
32 devices in a mesh: seq: 8 (over z, y), tp: 4 (over x, core).
Axes of the slice: x: 2, y: 2, z: 4, core: 2. Of those that a mesh axis runs over, the one named last changes fastest.
Arguments:
- inputs: bfloat16 [16, 1024, 768], P(None, 'seq'), may hold values from -6 to 6
- lengths: int32 [16], replicated, may hold values from 256 to 1024, as said below
- first_gain: float32 [768], replicated, may hold values from 0.5 to 1.5
- query_weight: bfloat16 [768, 768], P(None, 'tp'), may hold values from -0.21875 to 0.21875
- key_weight: bfloat16 [768, 768], P(None, 'tp'), may hold values from -0.21875 to 0.21875
- value_weight: bfloat16 [768, 768], P(None, 'tp'), may hold values from -0.21875 to 0.21875
- shift_taps: float32 [4, 768], P(None, 'tp'), may hold values from -3 to 3
- state_coef: float32 [768, 64], P('tp'), may hold values from -0.1875 to 0.1875
- state_rate: float32 [768, 64], P('tp'), may hold values from 0.00048828125 to 0.2
- skip_gain: float32 [768], P('tp'), may hold values from -3 to 3
- project_weight: bfloat16 [768, 768], P('tp'), may hold values from -0.21875 to 0.21875
- second_gain: float32 [768], replicated, may hold values from 0.5 to 1.5
- up_weight: bfloat16 [768, 3072], P(None, 'tp'), may hold values from -0.21875 to 0.21875
- down_weight: bfloat16 [3072, 768], P('tp'), may hold values from -0.109375 to 0.109375
- cotangent: bfloat16 [16, 1024, 768], P(None, 'seq'), may hold values from -6 to 6
Outputs:
- block_out: float32 [16, 1024, 768], P(None, 'seq')
- grad_inputs: float32 [16, 1024, 768], P(None, 'seq')
- grad_first: float32 [768], replicated
- grad_query: float32 [768, 768], P(None, 'tp')
- grad_key: float32 [768, 768], P(None, 'tp')
- grad_value: float32 [768, 768], P(None, 'tp')
- grad_taps: float32 [4, 768], P(None, 'tp')
- grad_coef: float32 [768, 64], P('tp')
- grad_rate: float32 [768, 64], P('tp')
- grad_skip: float32 [768], P('tp')
- grad_project: float32 [768, 768], P('tp')
- grad_second: float32 [768], replicated
- grad_up: float32 [768, 3072], P(None, 'tp')
- grad_down: float32 [3072, 768], P('tp')
Inputs may be any that keep to these rules, and one draw needn't show every extreme that they name: `lengths`: one of the 16 sequences, which one drawn from the seed, has exactly 1024 tokens; positions from a sequence's length on are padding.
All inputs are finite; a program needn't handle non-finite values.
Results may differ from a plain program's by a relative error of at most 0.0075.
Values sent between devices are 32-bit elements; how exact they have to be, the bound alone decides.
No kernel may reach another device: no remote copies, remote signals or barrier semaphores. Data moves between devices by JAX's collectives and lax.ppermute only.
A program may use at most 192 MiB of HBM per device.

v0:
```python
import jax
import jax.numpy as jnp
from jax import lax
from jax.sharding import PartitionSpec as P

exact_mode = lax.Precision.HIGHEST


def passed_along(x, axis, by):
    count = lax.axis_size(axis)
    pairs = [(i, i + by) for i in range(count) if 0 <= i + by < count]
    return lax.ppermute(x, axis, pairs)


def layer_norm(rows, gain):
    center = rows - jnp.mean(rows, axis=-1, keepdims=True)
    spread = jnp.mean(center * center, axis=-1, keepdims=True)
    return center * lax.rsqrt(spread + 1e-05) * gain


def kernel_values(coef, rate, freq, parity, total, length):
    half = jnp.pi * freq / total
    below = jnp.sin(half)
    square = (below * below)[:, None, None]
    whole = jnp.sin(2.0 * half)[:, None, None]
    decay = jnp.exp(-rate)
    gap = -jnp.expm1(-rate)
    ending = jnp.exp(-rate * length)
    numer = 1.0 - parity[:, None, None] * ending
    denom = gap * gap + 4.0 * decay * square
    real_term = numer * (gap + 2.0 * decay * square) / denom
    imag_term = -numer * decay * whole / denom
    return (jnp.sum(coef * real_term, axis=-1), jnp.sum(coef * imag_term, axis=-1))


def angles(left, right, modulus):
    return 2.0 * jnp.pi / modulus * (left[:, None] * right[None, :] % modulus).astype(jnp.float32)


def project(left, right):
    return jnp.einsum("btd,de->bte", left, right, preferred_element_type=jnp.float32)


def to_bins(signal, num_dev, place):
    num_seqs, block_len, channels = signal.shape
    per_dev = block_len // num_dev
    span_len = 2 * num_dev
    total = span_len * block_len
    parted = lax.all_to_all(
        signal.reshape(num_seqs, 1, block_len, channels),
        "seq",
        split_axis=2,
        concat_axis=1,
        tiled=True,
    )
    outer = angles(jnp.arange(num_dev), jnp.arange(span_len), span_len)
    first_re = jnp.einsum("bpmc,pq->bqmc", parted, jnp.cos(outer), precision=exact_mode)
    first_im = -jnp.einsum("bpmc,pq->bqmc", parted, jnp.sin(outer), precision=exact_mode)
    twist = angles(jnp.arange(span_len), place * per_dev + jnp.arange(per_dev), total)
    twist_cos = jnp.cos(twist)[None, :, :, None]
    twist_sin = jnp.sin(twist)[None, :, :, None]
    turned_re = first_re * twist_cos + first_im * twist_sin
    turned_im = first_im * twist_cos - first_re * twist_sin
    joined = lax.all_to_all(
        jnp.stack([turned_re, turned_im]), "seq", split_axis=2, concat_axis=3, tiled=True
    )
    wave = angles(jnp.arange(block_len), jnp.arange(block_len), block_len)
    wave_cos = jnp.cos(wave)
    wave_sin = jnp.sin(wave)
    spec_re = jnp.einsum("bqmc,mj->bqjc", joined[0], wave_cos, precision=exact_mode) + jnp.einsum(
        "bqmc,mj->bqjc", joined[1], wave_sin, precision=exact_mode
    )
    spec_im = jnp.einsum("bqmc,mj->bqjc", joined[1], wave_cos, precision=exact_mode) - jnp.einsum(
        "bqmc,mj->bqjc", joined[0], wave_sin, precision=exact_mode
    )
    return (spec_re, spec_im)


def from_bins(spec_re, spec_im, num_dev, place):
    num_seqs, bin_rows, block_len, channels = spec_re.shape
    span_len = 2 * num_dev
    total = span_len * block_len
    wave = angles(jnp.arange(block_len), jnp.arange(block_len), block_len)
    wave_cos = jnp.cos(wave)
    wave_sin = jnp.sin(wave)
    back_re = jnp.einsum("bqjc,jm->bqmc", spec_re, wave_cos, precision=exact_mode) - jnp.einsum(
        "bqjc,jm->bqmc", spec_im, wave_sin, precision=exact_mode
    )
    back_im = jnp.einsum("bqjc,jm->bqmc", spec_re, wave_sin, precision=exact_mode) + jnp.einsum(
        "bqjc,jm->bqmc", spec_im, wave_cos, precision=exact_mode
    )
    twist = angles(place * bin_rows + jnp.arange(bin_rows), jnp.arange(block_len), total)
    twist_cos = jnp.cos(twist)[None, :, :, None]
    twist_sin = jnp.sin(twist)[None, :, :, None]
    turned_re = back_re * twist_cos - back_im * twist_sin
    turned_im = back_re * twist_sin + back_im * twist_cos
    parted = lax.all_to_all(
        jnp.stack([turned_re, turned_im]), "seq", split_axis=3, concat_axis=2, tiled=True
    )
    outer = angles(jnp.arange(span_len), jnp.arange(num_dev), span_len)
    times_re = (
        jnp.einsum("bqmc,qp->bpmc", parted[0], jnp.cos(outer), precision=exact_mode)
        - jnp.einsum("bqmc,qp->bpmc", parted[1], jnp.sin(outer), precision=exact_mode)
    ) / total
    joined = lax.all_to_all(times_re, "seq", split_axis=1, concat_axis=2, tiled=True)
    return joined.reshape(num_seqs, block_len, channels)


def local(
    inputs,
    lengths,
    first_gain,
    query_weight,
    key_weight,
    value_weight,
    shift_taps,
    state_coef,
    state_rate,
    skip_gain,
    project_weight,
    second_gain,
    up_weight,
    down_weight,
    cotangent,
):
    num_dev = lax.axis_size("seq")
    place = lax.axis_index("seq")
    num_seqs, block_len, width_all = inputs.shape
    tap_count = shift_taps.shape[0]
    seq_len = num_dev * block_len
    total = 2 * seq_len
    source = inputs.astype(jnp.float32)
    positions = place * block_len + jnp.arange(block_len)
    validity = (positions[None, :] < lengths[:, None]).astype(jnp.float32)[:, :, None]
    normed = layer_norm(source, first_gain).astype(jnp.bfloat16)
    queries = project(normed, query_weight)
    key_rows = project(normed, key_weight)
    values = project(normed, value_weight)
    tail = key_rows[:, block_len - (tap_count - 1) :, :]
    before = passed_along(tail, "seq", 1)
    extended = jnp.concatenate([before, key_rows], axis=1)
    shifted = jnp.zeros_like(key_rows)
    for offset in range(tap_count):
        shifted = (
            shifted
            + shift_taps[offset]
            * extended[:, tap_count - 1 - offset : tap_count - 1 - offset + block_len, :]
        )
    mixed_in = shifted * values
    channels = state_coef.shape[0]
    bin_index = place * 2 + jnp.arange(2)
    freq_int = (bin_index[:, None] + 2 * num_dev * jnp.arange(block_len)[None, :]).reshape(-1)
    freq = freq_int.astype(jnp.float32)
    parity = (1 - 2 * (freq_int % 2)).astype(jnp.float32)

    def kernel_part(coef, rate):
        part_re, part_im = kernel_values(coef, rate, freq, parity, total, seq_len)
        return (part_re.reshape(2, block_len, channels), part_im.reshape(2, block_len, channels))

    (kernel_re, kernel_im), kernel_pull = jax.vjp(kernel_part, state_coef, state_rate)
    spec_re, spec_im = to_bins(mixed_in, num_dev, place)
    conv = from_bins(
        spec_re * kernel_re - spec_im * kernel_im,
        spec_re * kernel_im + spec_im * kernel_re,
        num_dev,
        place,
    )
    state_out = conv + skip_gain * mixed_in
    gated_out = (queries * state_out).astype(jnp.bfloat16)
    mixer = lax.psum(project(gated_out, project_weight), "tp")
    residual = source + mixer
    second = layer_norm(residual, second_gain).astype(jnp.bfloat16)
    up_act = project(second, up_weight)
    hidden = jax.nn.gelu(up_act).astype(jnp.bfloat16)
    lowered = lax.psum(project(hidden, down_weight), "tp")
    block_out = validity * (residual + lowered)
    d_mlp = validity * cotangent.astype(jnp.float32)
    d_mlp_low = d_mlp.astype(jnp.bfloat16)
    grad_down = jnp.einsum("btf,btd->fd", hidden, d_mlp_low, preferred_element_type=jnp.float32)
    d_hidden = jnp.einsum("btd,fd->btf", d_mlp_low, down_weight, preferred_element_type=jnp.float32)
    gelu_value, gelu_pull = jax.vjp(jax.nn.gelu, up_act)
    d_up = gelu_pull(d_hidden)[0].astype(jnp.bfloat16)
    grad_up = jnp.einsum("btd,btf->df", second, d_up, preferred_element_type=jnp.float32)
    d_second = lax.psum(
        jnp.einsum("btf,df->btd", d_up, up_weight, preferred_element_type=jnp.float32), "tp"
    )
    norm_value, second_pull = jax.vjp(layer_norm, residual, second_gain)
    d_resid_norm, grad_second = second_pull(d_second)
    d_residual = d_mlp + d_resid_norm
    d_resid_low = d_residual.astype(jnp.bfloat16)
    grad_project = jnp.einsum(
        "btc,btd->cd", gated_out, d_resid_low, preferred_element_type=jnp.float32
    )
    d_gated = jnp.einsum(
        "btd,cd->btc", d_resid_low, project_weight, preferred_element_type=jnp.float32
    )
    d_queries = (d_gated * state_out).astype(jnp.bfloat16)
    d_state = d_gated * queries
    back_re, back_im = to_bins(d_state, num_dev, place)
    fore_re, fore_im = to_bins(lax.optimization_barrier(mixed_in), num_dev, place)
    grad_kernel_re = jnp.sum(back_re * fore_re + back_im * fore_im, axis=0) / total
    grad_kernel_im = jnp.sum(back_im * fore_re - back_re * fore_im, axis=0) / total
    grad_coef, grad_rate = kernel_pull((grad_kernel_re, grad_kernel_im))
    corr = from_bins(
        back_re * kernel_re + back_im * kernel_im,
        back_im * kernel_re - back_re * kernel_im,
        num_dev,
        place,
    )
    d_mixed = corr + skip_gain * d_state
    grad_skip = jnp.sum(d_state * mixed_in, axis=(0, 1))
    d_values = (d_mixed * shifted).astype(jnp.bfloat16)
    d_shifted = d_mixed * values
    d_extended = jnp.zeros_like(extended)
    tap_sums = []
    for offset in range(tap_count):
        d_extended = d_extended + jnp.pad(
            shift_taps[offset] * d_shifted, ((0, 0), (tap_count - 1 - offset, offset), (0, 0))
        )
        tap_sums.append(
            jnp.sum(
                d_shifted
                * extended[:, tap_count - 1 - offset : tap_count - 1 - offset + block_len, :],
                axis=(0, 1),
            )
        )
    grad_taps = jnp.stack(tap_sums)
    spill = passed_along(d_extended[:, : tap_count - 1, :], "seq", -1)
    d_keys = (
        d_extended[:, tap_count - 1 :, :]
        + jnp.pad(spill, ((0, 0), (block_len - tap_count + 1, 0), (0, 0)))
    ).astype(jnp.bfloat16)
    grad_query = jnp.einsum("btd,btc->dc", normed, d_queries, preferred_element_type=jnp.float32)
    grad_key = jnp.einsum("btd,btc->dc", normed, d_keys, preferred_element_type=jnp.float32)
    grad_value = jnp.einsum("btd,btc->dc", normed, d_values, preferred_element_type=jnp.float32)
    d_first_part = jnp.einsum(
        "btc,dc->btd", d_queries, query_weight, preferred_element_type=jnp.float32
    )
    d_first_part = d_first_part + jnp.einsum(
        "btc,dc->btd", d_keys, key_weight, preferred_element_type=jnp.float32
    )
    d_first_part = d_first_part + jnp.einsum(
        "btc,dc->btd", d_values, value_weight, preferred_element_type=jnp.float32
    )
    d_first = lax.psum(d_first_part, "tp")
    first_value, first_pull = jax.vjp(layer_norm, source, first_gain)
    d_input_norm, grad_first = first_pull(d_first)
    grad_inputs = d_residual + d_input_norm
    (
        grad_first,
        grad_query,
        grad_key,
        grad_value,
        grad_taps,
        grad_coef,
        grad_rate,
        grad_skip,
        grad_project,
        grad_second,
        grad_up,
        grad_down,
    ) = lax.psum(
        (
            grad_first,
            grad_query,
            grad_key,
            grad_value,
            grad_taps,
            grad_coef,
            grad_rate,
            grad_skip,
            grad_project,
            grad_second,
            grad_up,
            grad_down,
        ),
        "seq",
    )
    return (
        block_out,
        grad_inputs,
        grad_first,
        grad_query,
        grad_key,
        grad_value,
        grad_taps,
        grad_coef,
        grad_rate,
        grad_skip,
        grad_project,
        grad_second,
        grad_up,
        grad_down,
    )


def solution(mesh):
    return jax.shard_map(
        local,
        mesh=mesh,
        in_specs=(
            P(None, "seq", None),
            P(),
            P(),
            P(None, "tp"),
            P(None, "tp"),
            P(None, "tp"),
            P(None, "tp"),
            P("tp", None),
            P("tp", None),
            P("tp"),
            P("tp", None),
            P(),
            P(None, "tp"),
            P("tp", None),
            P(None, "seq", None),
        ),
        out_specs=(
            P(None, "seq", None),
            P(None, "seq", None),
            P(),
            P(None, "tp"),
            P(None, "tp"),
            P(None, "tp"),
            P(None, "tp"),
            P("tp", None),
            P("tp", None),
            P("tp"),
            P("tp", None),
            P(),
            P(None, "tp"),
            P("tp", None),
        ),
        check_vma=False,
    )
```

profile of v0, /device:TPU:0, one launch (start us, length us, event | category | flops | bytes accessed | tf_op | source)
XLA Modules:
  0.0 2281.5 jit_solution(13198516228330018810)
XLA Ops:
  23.4 9.7 fusion.355
  42.4 46.5 %all-to-all-done = f32[16,1,128,192]{3,0,1,2:T(8,128)S(1)} async-done(((f32[16,1,128,192]{3,0,1,2:T(8,128)}), f32[16,1,128,192]{3,0,1,2:T(8,128)S(1)}, u32[]{:S(2)}, u32[]{:S(2)}) %all-to-all-start) | async-done | bytes 1572896 | tf_op jit(solution)/shard_map/all_to_all | solution.py:49
  100.1 8.3 copy.229
  114.4 14.0 multiply_reduce_fusion.7
  128.5 167.1 %all-to-all-done.1 = f32[2,16,16,16,192]{4,3,1,0,2:T(8,128)} async-done(((f32[2,16,16,16,192]{4,3,1,0,2:T(8,128)}), f32[2,16,16,16,192]{4,3,1,0,2:T(8,128)}, u32[]{:S(2)}, u32[]{:S(2)}) %all-to-all-start.1) | async-done | bytes 6291488 | tf_op jit(solution)/shard_map/all_to_all | solution.py:64
  347.2 12.7 copy.239
  359.9 186.8 %all_to_all.129 = f32[2,16,2,128,192]{4,2,1,0,3:T(2,128)S(1)} all-to-all(f32[2,16,2,128,192]{4,2,1,0,3:T(2,128)} %copy.239), channel_id=1, replica_groups=mesh['seq'=8,'tp'=4] {'seq'}, dimensions={3} | all-to-all | bytes 12582912 | tf_op jit(solution)/shard_map/all_to_all | solution.py:97
  586.6 51.4 %all_to_all.130 = f32[16,8,16,192]{3,2,0,1:T(8,128)S(1)} all-to-all(f32[16,8,16,192]{3,2,0,1:T(8,128)S(1)} %copy.243), channel_id=1, replica_groups=mesh['seq'=8,'tp'=4] {'seq'}, dimensions={1} | all-to-all | bytes 3145728 | tf_op jit(solution)/shard_map/all_to_all | solution.py:105
  652.8 117.9 %all-reduce.14.cloned.1.call-done = f32[16,128,768]{2,1,0:T(8,128)} async-done(((f32[16,128,768]{2,1,0:T(8,128)}), f32[16,128,768]{2,1,0:T(8,128)}) %all-reduce.14.cloned.1.call-update) | async-done | bytes 6291472 | tf_op jit(solution)/shard_map/psum | solution.py:170
  799.4 112.5 %all-reduce.16.cloned.1.call-done = f32[16,128,768]{2,1,0:T(8,128)} async-done(((f32[16,128,768]{2,1,0:T(8,128)}), f32[16,128,768]{2,1,0:T(8,128)}) %all-reduce.16.cloned.1.call-update) | async-done | bytes 6291472 | tf_op jit(solution)/shard_map/psum | solution.py:184
  953.3 35.3 %all-to-all-done.4 = f32[16,1,128,192]{3,0,1,2:T(8,128)} async-done(((f32[16,1,128,192]{3,0,1,2:T(8,128)}), f32[16,1,128,192]{3,0,1,2:T(8,128)}, u32[]{:S(2)}, u32[]{:S(2)}) %all-to-all-start.4) | async-done | bytes 1572896 | tf_op jit(solution)/shard_map/all_to_all | solution.py:49
  994.8 10.9 add_bitcast_fusion
  1033.1 169.4 %all-to-all-done.5 = f32[2,16,16,16,192]{4,3,1,0,2:T(8,128)} async-done(((f32[2,16,16,16,192]{4,3,1,0,2:T(8,128)}), f32[2,16,16,16,192]{4,3,1,0,2:T(8,128)}, u32[]{:S(2)}, u32[]{:S(2)}) %all-to-all-start.5) | async-done | bytes 6291488 | tf_op jit(solution)/shard_map/all_to_all | solution.py:64
  1259.4 12.7 copy.256
  1272.1 117.5 %all-to-all-done.9 = f32[2,16,16,16,192]{4,3,1,0,2:T(8,128)} async-done(((f32[2,16,16,16,192]{4,3,1,0,2:T(8,128)}), f32[2,16,16,16,192]{4,3,1,0,2:T(8,128)}, u32[]{:S(2)}, u32[]{:S(2)}) %all-to-all-start.9) | async-done | bytes 6291488 | tf_op jit(solution)/shard_map/all_to_all | solution.py:64
  1429.5 147.4 %all-to-all-done.6 = f32[2,16,2,128,192]{4,2,1,0,3:T(2,128)} async-done(((f32[2,16,2,128,192]{4,2,1,0,3:T(2,128)}), f32[2,16,2,128,192]{4,2,1,0,3:T(2,128)}, u32[]{:S(2)}, u32[]{:S(2)}) %all-to-all-start.6) | async-done | bytes 6291488 | tf_op jit(solution)/shard_map/all_to_all | solution.py:97
  1576.9 8.6 copy.257
  1661.4 12.7 all-to-all-done.7
  1680.2 8.6 multiply_reduce_fusion.14
  1713.3 35.0 %fusion.30 = (f32[192,64]{1,0:T(8,128)S(1)}, f32[192,64]{1,0:T(8,128)S(1)}, f32[192,64]{1,0:T(8,128)S(1)}, f32[192,64]{1,0:T(8,128)S(1)}, f32[192,64]{1,0:T(8,12...) fusion(f32[192,64]{1,0:T(8,128)S(1)} %copy-done.44, f32[192,64]{1,0:T(8,128)S(1)} %copy-done.48, ...), kind=kLoop, calls=%fused_computation.71 | loop fusion | flops 144605184 | bytes 1133568 | tf_op jit(solution)/shard_map/transpose(jvp())/reduce_sum | solution.py:30
  1755.2 178.1 %all-reduce.22.cloned.1.call-done = (f32[16,128,768]{2,1,0:T(8,128)}, f32[16,128,768]{2,1,0:T(8,128)}) async-done(((f32[16,128,768]{2,1,0:T(8,128)}, f32[16,128,768]{2,1,0:T(8,128)}), (f32[16,128,768]{2,1,0:T(8,128)}, f32[16,128,768]{2,1,0:T(8,128)})) %all-reduce.22.cloned.1.call-update) | async-done | bytes 12582928 | tf_op jit(solution)/shard_map/psum | solution.py:175
  1948.5 15.6 add_add_fusion.2
  1964.1 51.2 %all-reduce.18.cloned.1.call-done = (f32[768]{0:T(1024)}, f32[4,192]{1,0:T(4,128)}, f32[192,64]{1,0:T(8,128)}, f32[192,64]{1,0:T(8,128)}, f32[192]{0:T(256)}, /*index=5*/f32[768]{0:T(1024)}) async-done(((f32[768]{0:T(1024)}, f32[4,192]{1,0:T(4,128)}, f32[192,64]{1,0:T(8,128)}, f32[192,64]{1,0:T(8,128)}, f32[192]{0:T(256)}, /*index=5*/f32[768]{0:T(1024)}), (f32[768]{0:T(1024)}, f32[4,192]{1,0:T(4,128)}, ...) | async-done | bytes 108304 | tf_op jit(solution)/shard_map/psum | solution.py:262
  2018.5 241.1 %all-reduce.20.cloned.1.call-done = (f32[768,192]{0,1:T(8,128)}, f32[768,192]{0,1:T(8,128)}, f32[768,192]{0,1:T(8,128)}, f32[192,768]{1,0:T(8,128)}, f32[768,768]{1,0:T(8,128)}, /*index=5*/f32[768,768]{1,0:T(8,128)}) async-done(((f32[768,192]{0,1:T(8,128)}, f32[768,192]{0,1:T(8,128)}, f32[768,192]{0,1:T(8,128)}, f32[192,768]{1,0:T(8,128)}, f32[768,768]{1,0:T(8,128)}, /*index=5*/f32[768,768]{1,0:T(8,128)}), ...) | async-done | bytes 7077904 | tf_op jit(solution)/shard_map/psum | solution.py:262
  (368 shorter events, 494.8 us)
Async XLA Ops:
  7.2 768.8 %copy-start = (bf16[768,768]{1,0:T(8,128)(2,1)S(1)}, bf16[768,768]{1,0:T(8,128)(2,1)}, u32[]{:S(2)}) copy-start(bf16[768,768]{1,0:T(8,128)(2,1)} %param.27) | copy-start | bytes 3538948
  10.1 632.1 %copy-start.63 = (f32[16,128]{1,0:T(8,128)}, f32[16,128]{1,0:T(8,128)S(1)}, u32[]{:S(2)}) copy-start(f32[16,128]{1,0:T(8,128)S(1)} %broadcast_multiply_fusion.7) | copy-start | bytes 24580
  11.3 631.0 %copy-start.69 = (f32[16,128]{1,0:T(8,128)}, f32[16,128]{1,0:T(8,128)S(1)}, u32[]{:S(2)}) copy-start(f32[16,128]{1,0:T(8,128)S(1)} %fusion.170) | copy-start | bytes 24580
  15.1 6.6 collective-permute-start
  35.1 53.7 %all-to-all-start = ((f32[16,1,128,192]{3,0,1,2:T(8,128)}), f32[16,1,128,192]{3,0,1,2:T(8,128)S(1)}, u32[]{:S(2)}, u32[]{:S(2)}) async-start(f32[16,1,128,192]{3,0,1,2:T(8,128)} %copy.225), calls=%async_computation | async-start | bytes 4194304 | tf_op jit(solution)/shard_map/all_to_all | solution.py:49
  108.4 187.1 %all-to-all-start.1 = ((f32[2,16,16,16,192]{4,3,1,0,2:T(8,128)}), f32[2,16,16,16,192]{4,3,1,0,2:T(8,128)}, u32[]{:S(2)}, u32[]{:S(2)}) async-start(f32[2,16,16,16,192]{4,3,1,0,2:T(8,128)} %copy.229), calls=%async_computation.1 | async-start | bytes 16777216 | tf_op jit(solution)/shard_map/all_to_all | solution.py:64
  113.6 657.2 %all-reduce.14.cloned.1.call-start = ((), (), s32[]{:S(2)}) async-start(), calls=%async_computation.10 | async-start | bytes 12582912 | tf_op jit(solution)/shard_map/psum | solution.py:170
  114.1 225.7 %copy-start.81 = (f32[2,128]{1,0:T(2,128)}, f32[2,128]{1,0:T(2,128)S(1)}, u32[]{:S(2)}) copy-start(f32[2,128]{1,0:T(2,128)S(1)} %get-tuple-element.113) | copy-start | bytes 3076
  114.1 225.7 %copy-start.83 = (f32[2,128]{1,0:T(2,128)}, f32[2,128]{1,0:T(2,128)S(1)}, u32[]{:S(2)}) copy-start(f32[2,128]{1,0:T(2,128)S(1)} %get-tuple-element.114) | copy-start | bytes 3076
  128.5 211.3 %copy-start.18 = (f32[2,128,192]{1,2,0:T(8,128)}, f32[2,128,192]{1,2,0:T(8,128)S(1)}, u32[]{:S(2)}) copy-start(f32[2,128,192]{1,2,0:T(8,128)S(1)} %get-tuple-element.120) | copy-start | bytes 589828
  128.5 211.3 %copy-start.20 = (f32[2,128,192]{1,2,0:T(8,128)}, f32[2,128,192]{1,2,0:T(8,128)S(1)}, u32[]{:S(2)}) copy-start(f32[2,128,192]{1,2,0:T(8,128)S(1)} %get-tuple-element.121) | copy-start | bytes 589828
  652.1 259.8 %all-reduce.16.cloned.1.call-start = ((), (), s32[]{:S(2)}) async-start(), calls=%async_computation.11 | async-start | bytes 12582912 | tf_op jit(solution)/shard_map/psum | solution.py:184
  793.9 140.6 %all-to-all-start.8 = ((f32[16,1,128,192]{3,0,1,2:T(8,128)}), f32[16,1,128,192]{3,0,1,2:T(8,128)S(1)}, u32[]{:S(2)}, u32[]{:S(2)}) async-start(f32[16,1,128,192]{3,0,1,2:T(8,128)} %copy.265), calls=%async_computation.8 | async-start | bytes 4194304 | tf_op jit(solution)/shard_map/all_to_all | solution.py:49
  934.5 54.1 %all-to-all-start.4 = ((f32[16,1,128,192]{3,0,1,2:T(8,128)}), f32[16,1,128,192]{3,0,1,2:T(8,128)}, u32[]{:S(2)}, u32[]{:S(2)}) async-start(f32[16,1,128,192]{3,0,1,2:T(8,128)} %copy.246), calls=%async_computation.4 | async-start | bytes 4194304 | tf_op jit(solution)/shard_map/all_to_all | solution.py:49
  1015.5 187.0 %all-to-all-start.5 = ((f32[2,16,16,16,192]{4,3,1,0,2:T(8,128)}), f32[2,16,16,16,192]{4,3,1,0,2:T(8,128)}, u32[]{:S(2)}, u32[]{:S(2)}) async-start(f32[2,16,16,16,192]{4,3,1,0,2:T(8,128)} %copy.250), calls=%async_computation.5 | async-start | bytes 16777216 | tf_op jit(solution)/shard_map/all_to_all | solution.py:64
  1202.5 187.1 %all-to-all-start.9 = ((f32[2,16,16,16,192]{4,3,1,0,2:T(8,128)}), f32[2,16,16,16,192]{4,3,1,0,2:T(8,128)}, u32[]{:S(2)}, u32[]{:S(2)}) async-start(f32[2,16,16,16,192]{4,3,1,0,2:T(8,128)} %copy.269), calls=%async_computation.9 | async-start | bytes 16777216 | tf_op jit(solution)/shard_map/all_to_all | solution.py:64
  1389.6 187.3 %all-to-all-start.6 = ((f32[2,16,2,128,192]{4,2,1,0,3:T(2,128)}), f32[2,16,2,128,192]{4,2,1,0,3:T(2,128)}, u32[]{:S(2)}, u32[]{:S(2)}) async-start(f32[2,16,2,128,192]{4,2,1,0,3:T(2,128)} %copy.256), calls=%async_computation.6 | async-start | bytes 16777216 | tf_op jit(solution)/shard_map/all_to_all | solution.py:97
  1621.8 52.4 %all-to-all-start.7 = ((f32[16,8,16,192]{3,2,0,1:T(8,128)}), f32[16,8,16,192]{3,2,0,1:T(8,128)}, u32[]{:S(2)}, u32[]{:S(2)}) async-start(f32[16,8,16,192]{3,2,0,1:T(8,128)} %copy.260), calls=%async_computation.7 | async-start | bytes 4194304 | tf_op jit(solution)/shard_map/all_to_all | solution.py:105
  1626.1 307.2 %all-reduce.22.cloned.1.call-start = ((), (), s32[]{:S(2)}) async-start(), calls=%async_computation.14 | async-start | bytes 25165824 | tf_op jit(solution)/shard_map/psum | solution.py:175
  1694.4 6.0 collective-permute-start.1
  1712.1 303.3 %all-reduce.18.cloned.1.call-start = ((), (), s32[]{:S(2)}) async-start(), calls=%async_computation.12 | async-start | bytes 419840 | tf_op jit(solution)/shard_map/psum | solution.py:262
  1751.0 182.3 %copy-start.76 = (f32[768]{0:T(1024)S(1)}, f32[768]{0:T(1024)}, u32[]{:S(2)}) copy-start(f32[768]{0:T(1024)} %param.17) | copy-start | bytes 9220
  1943.7 316.0 %all-reduce.20.cloned.1.call-start = ((), (), s32[]{:S(2)}) async-start(), calls=%async_computation.13 | async-start | bytes 14155776 | tf_op jit(solution)/shard_map/psum | solution.py:262
  2015.3 256.1 %copy-start.96 = (f32[768]{0:T(1024)S(1)}, f32[768]{0:T(1024)}, u32[]{:S(2)}) copy-start(f32[768]{0:T(1024)} %get-tuple-element.133) | copy-start | bytes 9220
  (95 other events, 648.5 us)
Sparse Core Ops, SparseCore 0:
  652.2 118.4 all-reduce.13
  792.1 119.7 all-reduce.15
  1712.2 221.1 all-reduce.21
  1943.8 71.4 all-reduce.17
  2022.2 237.4 all-reduce.19
where the time goes:
time: 2290 us; the launch traced here: 2280 us
  waiting for transfers between devices  1400 us (61%)
  matrix products  252 us (11%)
  blocking collectives  238 us (10%)
  local copies, waits for them, and re-layouts  198 us (9%)
  other arithmetic  128 us (6%)
  starting transfers between devices  50.5 us (2%)
    all_to_all x3, waiting for transfers between devices, to_bins(): lax.all_to_all(jnp.stack([turned_re, turned_im]), 'seq', split_axis=2, co...  454 us
    psum x2, waiting for transfers between devices, local(): lax.psum((grad_first, grad_query, grad_key, grad_value, grad_taps, grad_c...  292 us
    all_to_all x1, blocking collectives, from_bins(): lax.all_to_all(jnp.stack([turned_re, turned_im]), 'seq', split_axis=3, co...  187 us
    psum x1, waiting for transfers between devices, local(): lowered = lax.psum(project(hidden, down_weight), 'tp')  178 us
    all_to_all x1, waiting for transfers between devices, from_bins(): lax.all_to_all(jnp.stack([turned_re, turned_im]), 'seq', split_axis=3, co...  147 us
    psum x1, waiting for transfers between devices, local(): mixer = lax.psum(project(gated_out, project_weight), 'tp')  118 us
    psum x1, waiting for transfers between devices, local(): lax.psum(jnp.einsum('btf,df->btd', d_up, up_weight, preferred_element_typ...  113 us
    all_to_all x3, waiting for transfers between devices, to_bins(): lax.all_to_all(signal.reshape(num_seqs, 1, block_len, channels), 'seq', s...  81.8 us
  transfers between devices with their start and end apart: 15, of which 14 were waited for; matrix products, arithmetic and copies ran while one was open for 11% of the time, Pallas kernels for 0%

commit v1 on v0

--- a/solution.py
+++ b/solution.py
@@ -102,7 +102,23 @@
         jnp.einsum("bqmc,qp->bpmc", parted[0], jnp.cos(outer), precision=exact_mode)
         - jnp.einsum("bqmc,qp->bpmc", parted[1], jnp.sin(outer), precision=exact_mode)
     ) / total
-    joined = lax.all_to_all(times_re, "seq", split_axis=1, concat_axis=2, tiled=True)
+    mixed_arr = lax.axis_size("seq")
+    frame_out = lax.axis_index("seq")
+    local_out, y = (mixed_arr, frame_out)
+    all_rows = list(times_re.shape)
+    main = times_re.shape[1] // local_out
+    all_rows[1] = main
+    reply = all_rows[2]
+    all_rows[2] = reply * local_out
+    joined = jnp.zeros(all_rows, times_re.dtype)
+    for t in tuple(range(local_out)):
+        all_values = lax.dynamic_slice_in_dim(times_re, (y ^ t) * main, main, axis=1)
+        if t:
+            cards = []
+            for dd in [*range(local_out)]:
+                cards.append((dd, dd ^ t))
+            all_values = lax.ppermute(all_values, axis_name="seq", perm=cards)
+        joined = lax.dynamic_update_slice_in_dim(joined, all_values, (y ^ t) * reply, axis=2)
     return joined.reshape(num_seqs, block_len, channels)
 
 

time: 2290 us -> 2410 us (1.052)
  blocking collectives: 238 us -> 0 us
  local copies, waits for them, and re-layouts: 198 us -> 376 us
  waiting for transfers between devices: 1400 us -> 1550 us
    all_to_all x2 -> x0, blocking collectives: 238 us -> none  [the longest x1 187 us: from_bins(): lax.all_to_all(jnp.stack([turned_re, turned_im]), 'seq', split_axis=3, co...]
    dynamic_update_slice x0 -> x16, local copies, waits for them, and re-layouts: none -> 162 us  [from_bins(): lax.dynamic_update_slice_in_dim(joined, all_values, (y ^ t) * reply, axis=2)]
    all_to_all x1 -> x2, waiting for transfers between devices: 147 us -> 297 us  [from_bins(): lax.all_to_all(jnp.stack([turned_re, turned_im]), 'seq', split_axis=3, co...]
  transfers between devices with their start and end apart: 15 -> 29, of which waited for: 14 -> 16; matrix products, arithmetic and copies ran while one was open for 11% -> 18% of each run, Pallas kernels for 0% -> 0%
where the time goes in v1:
time: 2410 us; the launch traced here: 2400 us
  waiting for transfers between devices  1550 us (64%)
  local copies, waits for them, and re-layouts  376 us (16%)
  matrix products  256 us (11%)
  other arithmetic  127 us (5%)
  starting transfers between devices  70.1 us (3%)
    all_to_all x3, waiting for transfers between devices, to_bins(): lax.all_to_all(jnp.stack([turned_re, turned_im]), 'seq', split_axis=2, co...  454 us
    all_to_all x2, waiting for transfers between devices, from_bins(): lax.all_to_all(jnp.stack([turned_re, turned_im]), 'seq', split_axis=3, co...  297 us
    psum x2, waiting for transfers between devices, local(): lax.psum((grad_first, grad_query, grad_key, grad_value, grad_taps, grad_c...  292 us
    psum x1, waiting for transfers between devices, local(): lowered = lax.psum(project(hidden, down_weight), 'tp')  180 us
    dynamic_update_slice x16, local copies, waits for them, and re-layouts, from_bins(): lax.dynamic_update_slice_in_dim(joined, all_values, (y ^ t) * reply, axis=2)  162 us
    psum x1, waiting for transfers between devices, local(): mixer = lax.psum(project(gated_out, project_weight), 'tp')  121 us
    psum x1, waiting for transfers between devices, local(): lax.psum(jnp.einsum('btf,df->btd', d_up, up_weight, preferred_element_typ...  113 us
    all_to_all x3, waiting for transfers between devices, to_bins(): lax.all_to_all(signal.reshape(num_seqs, 1, block_len, channels), 'seq', s...  82 us
  transfers between devices with their start and end apart: 29, of which 16 were waited for; matrix products, arithmetic and copies ran while one was open for 18% of the time, Pallas kernels for 0%

profile of v1, /device:TPU:0, one launch (start us, length us, event | category | flops | bytes accessed | tf_op | source)
XLA Modules:
  0.0 2398.8 jit_solution(7498581911325396673)
XLA Ops:
  42.0 46.7 %all-to-all-done = f32[16,1,128,192]{3,0,1,2:T(8,128)S(1)} async-done(((f32[16,1,128,192]{3,0,1,2:T(8,128)}), f32[16,1,128,192]{3,0,1,2:T(8,128)S(1)}, u32[]{:S(2)}, u32[]{:S(2)}) %all-to-all-start) | async-done | bytes 1572896 | tf_op jit(solution)/shard_map/all_to_all | solution.py:49
  114.5 14.0 multiply_reduce_fusion.7
  128.6 167.2 %all-to-all-done.1 = f32[2,16,16,16,192]{4,3,1,0,2:T(8,128)} async-done(((f32[2,16,16,16,192]{4,3,1,0,2:T(8,128)}), f32[2,16,16,16,192]{4,3,1,0,2:T(8,128)}, u32[]{:S(2)}, u32[]{:S(2)}) %all-to-all-start.1) | async-done | bytes 6291488 | tf_op jit(solution)/shard_map/all_to_all | solution.py:64
  347.2 12.7 copy.285
  365.0 181.8 %all-to-all-done.2 = f32[2,16,2,128,192]{4,2,1,0,3:T(2,128)} async-done(((f32[2,16,2,128,192]{4,2,1,0,3:T(2,128)}), f32[2,16,2,128,192]{4,2,1,0,3:T(2,128)}, u32[]{:S(2)}, u32[]{:S(2)}) %all-to-all-start.2) | async-done | bytes 6291488 | tf_op jit(solution)/shard_map/all_to_all | solution.py:97
  622.6 10.7 dynamic_update_slice.65
  634.7 10.9 dynamic_update_slice.66
  647.1 10.7 dynamic_update_slice.67
  659.2 10.7 dynamic_update_slice.68
  670.4 10.7 dynamic_update_slice.69
  715.7 120.5 %all-reduce.14.cloned.1.call-done = f32[16,128,768]{2,1,0:T(8,128)} async-done(((f32[16,128,768]{2,1,0:T(8,128)}), f32[16,128,768]{2,1,0:T(8,128)}) %all-reduce.14.cloned.1.call-update) | async-done | bytes 6291472 | tf_op jit(solution)/shard_map/psum | solution.py:186
  865.1 112.5 %all-reduce.16.cloned.1.call-done = f32[16,128,768]{2,1,0:T(8,128)} async-done(((f32[16,128,768]{2,1,0:T(8,128)}), f32[16,128,768]{2,1,0:T(8,128)}) %all-reduce.16.cloned.1.call-update) | async-done | bytes 6291472 | tf_op jit(solution)/shard_map/psum | solution.py:200
  1018.9 35.3 %all-to-all-done.3 = f32[16,1,128,192]{3,0,1,2:T(8,128)} async-done(((f32[16,1,128,192]{3,0,1,2:T(8,128)}), f32[16,1,128,192]{3,0,1,2:T(8,128)}, u32[]{:S(2)}, u32[]{:S(2)}) %all-to-all-start.3) | async-done | bytes 1572896 | tf_op jit(solution)/shard_map/all_to_all | solution.py:49
  1060.4 10.9 add_bitcast_fusion
  1098.7 169.4 %all-to-all-done.4 = f32[2,16,16,16,192]{4,3,1,0,2:T(8,128)} async-done(((f32[2,16,16,16,192]{4,3,1,0,2:T(8,128)}), f32[2,16,16,16,192]{4,3,1,0,2:T(8,128)}, u32[]{:S(2)}, u32[]{:S(2)}) %all-to-all-start.4) | async-done | bytes 6291488 | tf_op jit(solution)/shard_map/all_to_all | solution.py:64
  1324.8 12.7 copy.307
  1337.5 117.6 %all-to-all-done.7 = f32[2,16,16,16,192]{4,3,1,0,2:T(8,128)} async-done(((f32[2,16,16,16,192]{4,3,1,0,2:T(8,128)}), f32[2,16,16,16,192]{4,3,1,0,2:T(8,128)}, u32[]{:S(2)}, u32[]{:S(2)}) %all-to-all-start.7) | async-done | bytes 6291488 | tf_op jit(solution)/shard_map/all_to_all | solution.py:64
  1526.9 115.6 %all-to-all-done.5 = f32[2,16,2,128,192]{4,2,1,0,3:T(2,128)} async-done(((f32[2,16,2,128,192]{4,2,1,0,3:T(2,128)}), f32[2,16,2,128,192]{4,2,1,0,3:T(2,128)}, u32[]{:S(2)}, u32[]{:S(2)}) %all-to-all-start.5) | async-done | bytes 6291488 | tf_op jit(solution)/shard_map/all_to_all | solution.py:97
  1728.5 10.9 dynamic_update_slice.74
  1828.6 35.0 %fusion.30 = (f32[192,64]{1,0:T(8,128)S(1)}, f32[192,64]{1,0:T(8,128)S(1)}, f32[192,64]{1,0:T(8,128)S(1)}, f32[192,64]{1,0:T(8,128)S(1)}, f32[192,64]{1,0:T(8,12...) fusion(f32[192,64]{1,0:T(8,128)S(1)} %copy-done.44, f32[192,64]{1,0:T(8,128)S(1)} %copy-done.48, ...), kind=kLoop, calls=%fused_computation.71 | loop fusion | flops 144605184 | bytes 1133568 | tf_op jit(solution)/shard_map/transpose(jvp())/reduce_sum | solution.py:30
  1870.5 179.9 %all-reduce.22.cloned.1.call-done = (f32[16,128,768]{2,1,0:T(8,128)}, f32[16,128,768]{2,1,0:T(8,128)}) async-done(((f32[16,128,768]{2,1,0:T(8,128)}, f32[16,128,768]{2,1,0:T(8,128)}), (f32[16,128,768]{2,1,0:T(8,128)}, f32[16,128,768]{2,1,0:T(8,128)})) %all-reduce.22.cloned.1.call-update) | async-done | bytes 12582928 | tf_op jit(solution)/shard_map/psum | solution.py:191
  2065.5 15.6 add_add_fusion.2
  2081.1 51.3 %all-reduce.18.cloned.1.call-done = (f32[768]{0:T(1024)}, f32[4,192]{1,0:T(4,128)}, f32[192,64]{1,0:T(8,128)}, f32[192,64]{1,0:T(8,128)}, f32[192]{0:T(256)}, /*index=5*/f32[768]{0:T(1024)}) async-done(((f32[768]{0:T(1024)}, f32[4,192]{1,0:T(4,128)}, f32[192,64]{1,0:T(8,128)}, f32[192,64]{1,0:T(8,128)}, f32[192]{0:T(256)}, /*index=5*/f32[768]{0:T(1024)}), (f32[768]{0:T(1024)}, f32[4,192]{1,0:T(4,128)}, ...) | async-done | bytes 108304 | tf_op jit(solution)/shard_map/psum | solution.py:278
  2135.6 241.1 %all-reduce.20.cloned.1.call-done = (f32[768,192]{0,1:T(8,128)}, f32[768,192]{0,1:T(8,128)}, f32[768,192]{0,1:T(8,128)}, f32[192,768]{1,0:T(8,128)}, f32[768,768]{1,0:T(8,128)}, /*index=5*/f32[768,768]{1,0:T(8,128)}) async-done(((f32[768,192]{0,1:T(8,128)}, f32[768,192]{0,1:T(8,128)}, f32[768,192]{0,1:T(8,128)}, f32[192,768]{1,0:T(8,128)}, f32[768,768]{1,0:T(8,128)}, /*index=5*/f32[768,768]{1,0:T(8,128)}), ...) | async-done | bytes 7077904 | tf_op jit(solution)/shard_map/psum | solution.py:278
  (464 shorter events, 678.4 us)
Async XLA Ops:
  35.0 53.8 %all-to-all-start = ((f32[16,1,128,192]{3,0,1,2:T(8,128)}), f32[16,1,128,192]{3,0,1,2:T(8,128)S(1)}, u32[]{:S(2)}, u32[]{:S(2)}) async-start(f32[16,1,128,192]{3,0,1,2:T(8,128)} %copy.271), calls=%async_computation | async-start | bytes 4194304 | tf_op jit(solution)/shard_map/all_to_all | solution.py:49
  108.7 187.1 %all-to-all-start.1 = ((f32[2,16,16,16,192]{4,3,1,0,2:T(8,128)}), f32[2,16,16,16,192]{4,3,1,0,2:T(8,128)}, u32[]{:S(2)}, u32[]{:S(2)}) async-start(f32[2,16,16,16,192]{4,3,1,0,2:T(8,128)} %copy.275), calls=%async_computation.1 | async-start | bytes 16777216 | tf_op jit(solution)/shard_map/all_to_all | solution.py:64
  359.9 186.9 %all-to-all-start.2 = ((f32[2,16,2,128,192]{4,2,1,0,3:T(2,128)}), f32[2,16,2,128,192]{4,2,1,0,3:T(2,128)}, u32[]{:S(2)}, u32[]{:S(2)}) async-start(f32[2,16,2,128,192]{4,2,1,0,3:T(2,128)} %copy.285), calls=%async_computation.2 | async-start | bytes 16777216 | tf_op jit(solution)/shard_map/all_to_all | solution.py:97
  364.9 471.4 %all-reduce.14.cloned.1.call-start = ((), (), s32[]{:S(2)}) async-start(), calls=%async_computation.8 | async-start | bytes 12582912 | tf_op jit(solution)/shard_map/psum | solution.py:186
  593.4 17.4 collective-permute-start.2
  594.2 51.4 %collective-permute-start.3 = (f32[16,1,16,192]{3,2,1,0:T(8,128)}, f32[16,1,16,192]{3,2,1,0:T(8,128)}, u32[]{:S(2)}, u32[]{:S(2)}) collective-permute-start(f32[16,1,16,192]{3,2,1,0:T(8,128)} %bitcast.446), channel_id=1, source_target_pairs={{0,12},{4,8},{8,4},{12,0},{16,28},{20,24},{24,20},{28,16},{1,13},{... | collective-permute-start | bytes 589832 | tf_op jit(solution)/shard_map/ppermute | solution.py:120
  596.9 60.8 %collective-permute-start.4 = (f32[16,1,16,192]{3,2,1,0:T(8,128)}, f32[16,1,16,192]{3,2,1,0:T(8,128)}, u32[]{:S(2)}, u32[]{:S(2)}) collective-permute-start(f32[16,1,16,192]{3,2,1,0:T(8,128)} %bitcast.445), channel_id=1, source_target_pairs={{0,16},{4,20},{8,24},{12,28},{16,0},{20,4},{24,8},{28,12},{1,17},{... | collective-permute-start | bytes 589832 | tf_op jit(solution)/shard_map/ppermute | solution.py:120
  598.9 71.1 %collective-permute-start.5 = (f32[16,1,16,192]{3,2,1,0:T(8,128)}, f32[16,1,16,192]{3,2,1,0:T(8,128)S(1)}, u32[]{:S(2)}, u32[]{:S(2)}) collective-permute-start(f32[16,1,16,192]{3,2,1,0:T(8,128)} %bitcast.444), channel_id=1, source_target_pairs={{0,20},{4,16},{8,28},{12,24},{16,4},{20,0},{24,12},{28,8},{1,21},{... | collective-permute-start | bytes 589832 | tf_op jit(solution)/shard_map/ppermute | solution.py:120
  602.2 78.9 %collective-permute-start.6 = (f32[16,1,16,192]{3,2,1,0:T(8,128)}, f32[16,1,16,192]{3,2,1,0:T(8,128)S(1)}, u32[]{:S(2)}, u32[]{:S(2)}) collective-permute-start(f32[16,1,16,192]{3,2,1,0:T(8,128)} %bitcast.443), channel_id=1, source_target_pairs={{0,24},{4,28},{8,16},{12,20},{16,8},{20,12},{24,0},{28,4},{1,25},{... | collective-permute-start | bytes 589832 | tf_op jit(solution)/shard_map/ppermute | solution.py:120
  611.5 81.2 %collective-permute-start.7 = (f32[16,1,16,192]{3,2,1,0:T(8,128)}, f32[16,1,16,192]{3,2,1,0:T(8,128)}, u32[]{:S(2)}, u32[]{:S(2)}) collective-permute-start(f32[16,1,16,192]{3,2,1,0:T(8,128)} %bitcast.442), channel_id=1, source_target_pairs={{0,28},{4,24},{8,20},{12,16},{16,12},{20,8},{24,4},{28,0},{1,29},{... | collective-permute-start | bytes 589832 | tf_op jit(solution)/shard_map/ppermute | solution.py:120
  715.0 262.6 %all-reduce.16.cloned.1.call-start = ((), (), s32[]{:S(2)}) async-start(), calls=%async_computation.9 | async-start | bytes 12582912 | tf_op jit(solution)/shard_map/psum | solution.py:200
  859.6 140.6 %all-to-all-start.6 = ((f32[16,1,128,192]{3,0,1,2:T(8,128)}), f32[16,1,128,192]{3,0,1,2:T(8,128)S(1)}, u32[]{:S(2)}, u32[]{:S(2)}) async-start(f32[16,1,128,192]{3,0,1,2:T(8,128)} %copy.321), calls=%async_computation.6 | async-start | bytes 4194304 | tf_op jit(solution)/shard_map/all_to_all | solution.py:49
  1000.2 54.0 %all-to-all-start.3 = ((f32[16,1,128,192]{3,0,1,2:T(8,128)}), f32[16,1,128,192]{3,0,1,2:T(8,128)}, u32[]{:S(2)}, u32[]{:S(2)}) async-start(f32[16,1,128,192]{3,0,1,2:T(8,128)} %copy.297), calls=%async_computation.3 | async-start | bytes 4194304 | tf_op jit(solution)/shard_map/all_to_all | solution.py:49
  1081.1 187.0 %all-to-all-start.4 = ((f32[2,16,16,16,192]{4,3,1,0,2:T(8,128)}), f32[2,16,16,16,192]{4,3,1,0,2:T(8,128)}, u32[]{:S(2)}, u32[]{:S(2)}) async-start(f32[2,16,16,16,192]{4,3,1,0,2:T(8,128)} %copy.301), calls=%async_computation.4 | async-start | bytes 16777216 | tf_op jit(solution)/shard_map/all_to_all | solution.py:64
  1268.1 187.1 %all-to-all-start.7 = ((f32[2,16,16,16,192]{4,3,1,0,2:T(8,128)}), f32[2,16,16,16,192]{4,3,1,0,2:T(8,128)}, u32[]{:S(2)}, u32[]{:S(2)}) async-start(f32[2,16,16,16,192]{4,3,1,0,2:T(8,128)} %copy.325), calls=%async_computation.7 | async-start | bytes 16777216 | tf_op jit(solution)/shard_map/all_to_all | solution.py:64
  1455.2 187.3 %all-to-all-start.5 = ((f32[2,16,2,128,192]{4,2,1,0,3:T(2,128)}), f32[2,16,2,128,192]{4,2,1,0,3:T(2,128)}, u32[]{:S(2)}, u32[]{:S(2)}) async-start(f32[2,16,2,128,192]{4,2,1,0,3:T(2,128)} %copy.307), calls=%async_computation.5 | async-start | bytes 16777216 | tf_op jit(solution)/shard_map/all_to_all | solution.py:97
  1460.1 590.2 %all-reduce.22.cloned.1.call-start = ((), (), s32[]{:S(2)}) async-start(), calls=%async_computation.12 | async-start | bytes 25165824 | tf_op jit(solution)/shard_map/psum | solution.py:191
  1690.2 49.2 %collective-permute-start.10 = (f32[16,1,16,192]{3,2,1,0:T(8,128)}, f32[16,1,16,192]{3,2,1,0:T(8,128)S(1)}, u32[]{:S(2)}, u32[]{:S(2)}) collective-permute-start(f32[16,1,16,192]{3,2,1,0:T(8,128)} %bitcast.439), channel_id=1, source_target_pairs={{0,12},{4,8},{8,4},{12,0},{16,28},{20,24},{24,20},{28,16},{1,13},{... | collective-permute-start | bytes 589832 | tf_op jit(solution)/shard_map/ppermute | solution.py:120
  1692.9 57.7 %collective-permute-start.11 = (f32[16,1,16,192]{3,2,1,0:T(8,128)}, f32[16,1,16,192]{3,2,1,0:T(8,128)S(1)}, u32[]{:S(2)}, u32[]{:S(2)}) collective-permute-start(f32[16,1,16,192]{3,2,1,0:T(8,128)} %bitcast.438), channel_id=1, source_target_pairs={{0,16},{4,20},{8,24},{12,28},{16,0},{20,4},{24,8},{28,12},{1,17},{... | collective-permute-start | bytes 589832 | tf_op jit(solution)/shard_map/ppermute | solution.py:120
  1694.9 67.0 %collective-permute-start.12 = (f32[16,1,16,192]{3,2,1,0:T(8,128)}, f32[16,1,16,192]{3,2,1,0:T(8,128)S(1)}, u32[]{:S(2)}, u32[]{:S(2)}) collective-permute-start(f32[16,1,16,192]{3,2,1,0:T(8,128)} %bitcast.437), channel_id=1, source_target_pairs={{0,20},{4,16},{8,28},{12,24},{16,4},{20,0},{24,12},{28,8},{1,21},{... | collective-permute-start | bytes 589832 | tf_op jit(solution)/shard_map/ppermute | solution.py:120
  1698.9 74.1 %collective-permute-start.13 = (f32[16,1,16,192]{3,2,1,0:T(8,128)}, f32[16,1,16,192]{3,2,1,0:T(8,128)S(1)}, u32[]{:S(2)}, u32[]{:S(2)}) collective-permute-start(f32[16,1,16,192]{3,2,1,0:T(8,128)} %bitcast.436), channel_id=1, source_target_pairs={{0,24},{4,28},{8,16},{12,20},{16,8},{20,12},{24,0},{28,4},{1,25},{... | collective-permute-start | bytes 589832 | tf_op jit(solution)/shard_map/ppermute | solution.py:120
  1705.4 79.2 %collective-permute-start.14 = (f32[16,1,16,192]{3,2,1,0:T(8,128)}, f32[16,1,16,192]{3,2,1,0:T(8,128)S(1)}, u32[]{:S(2)}, u32[]{:S(2)}) collective-permute-start(f32[16,1,16,192]{3,2,1,0:T(8,128)} %bitcast.435), channel_id=1, source_target_pairs={{0,28},{4,24},{8,20},{12,16},{16,12},{20,8},{24,4},{28,0},{1,29},{... | collective-permute-start | bytes 589832 | tf_op jit(solution)/shard_map/ppermute | solution.py:120
  1827.4 305.0 %all-reduce.18.cloned.1.call-start = ((), (), s32[]{:S(2)}) async-start(), calls=%async_computation.10 | async-start | bytes 419840 | tf_op jit(solution)/shard_map/psum | solution.py:278
  2060.7 316.0 %all-reduce.20.cloned.1.call-start = ((), (), s32[]{:S(2)}) async-start(), calls=%async_computation.11 | async-start | bytes 14155776 | tf_op jit(solution)/shard_map/psum | solution.py:278
  (122 other events, 4572.2 us)
Sparse Core Ops, SparseCore 0:
  715.1 121.0 all-reduce.13
  857.8 119.7 all-reduce.15
  1827.5 222.7 all-reduce.21
  2060.9 71.4 all-reduce.17
  2139.2 237.4 all-reduce.19
